TPU v7x, 32 devices: a whole 2x2x4 slice. The times are simulated.
32 devices in a mesh: aux: 4 (over y, x), blk: 8 (over z, core).
Axes of the slice: x: 2, y: 2, z: 4, core: 2. Of those that a mesh axis runs over, the one named last changes fastest.
Arguments:
- three_center: bfloat16 [384, 4, 128, 128], P(('aux', 'blk')), may hold values from -6 to 6
- slot_block: int32 [384], P(('aux', 'blk')), may hold values from 0 to 47
- slot_aux: int32 [384], P(('aux', 'blk')), may hold values from 0 to 1
- live_slots: int32 [32], P(('aux', 'blk')), may hold values from 1 to 12, as said below
- vir_coef: bfloat16 [6144, 256], replicated, may hold values from -0.00478416 to 0.00478416
- eps_occ: float32 [4000], replicated, may hold values from -1.5 to -0.3
- eps_vir: float32 [256], replicated, may hold values from 0.2 to 3
- occ_index: int32 [4], replicated, may hold values from 0 to 3999, as said below
Outputs:
- amplitudes: float32 [4, 256, 4, 256], P('aux', 'blk')
- pair_energy: float32 [4, 4], P('aux')
Inputs may be any that keep to these rules, and one draw needn't show every extreme that they name: The slots in use on a device are its first live_slots ones; the others hold data that is not used. Some device holds exactly 12 slots in use in every draw. `occ_index`: the indices are distinct; the first and the last occupied orbital of the system are in every batch.
All inputs are finite; a program needn't handle non-finite values.
Results may differ from a plain program's by a relative error of at most 0.0035.
Values may be sent and summed in bfloat16 or wider, within the bound.
A program may use at most 64 MiB of HBM per device.

v0:
```python
import jax
import jax.numpy as jnp
from jax import lax
from jax.sharding import PartitionSpec as P

AUX_BLOCKS_DEV = 2


def body(three_center, slot_block, slot_aux, live_slots, vir_coef, eps_occ, eps_vir, occ_index):
    blk_count = lax.axis_size("blk")
    occ_row = lax.axis_index("aux")
    slot_count = three_center.shape[0]
    occ_count = three_center.shape[1]
    ao_span = three_center.shape[3]
    vir_count = vir_coef.shape[1]
    coef_blocks = vir_coef.reshape(vir_coef.shape[0] // ao_span, ao_span, vir_count)
    coefficients = jnp.take(coef_blocks, slot_block, axis=0)
    products = jnp.einsum(
        "soqn,snv->soqv", three_center, coefficients, preferred_element_type=jnp.float32
    )
    keep = (jnp.arange(slot_count) < live_slots[0]).astype(jnp.float32)
    select = (slot_aux[:, None] == jnp.arange(AUX_BLOCKS_DEV)[None, :]).astype(jnp.float32)
    select = select * keep[:, None]
    local_rows = jnp.einsum("sk,soqv->kqov", select, products).astype(jnp.bfloat16)
    halfed = lax.all_gather(local_rows, "aux", axis=0, tiled=True)
    own_rows = lax.dynamic_index_in_dim(halfed, occ_row, 2, keepdims=False)
    rows_dev = vir_count // blk_count
    mixed = lax.dot_general(
        halfed, own_rows, (((0, 1), (0, 1)), ((), ())), preferred_element_type=jnp.float32
    )
    summed = lax.psum_scatter(
        jnp.stack(
            [
                lax.dot_general(
                    own_rows,
                    halfed,
                    (((0, 1), (0, 1)), ((), ())),
                    preferred_element_type=jnp.float32,
                ),
                jnp.transpose(mixed, (1, 0, 2)),
            ],
            axis=1,
        ),
        "blk",
        scatter_dimension=0,
        tiled=True,
    )
    direct = summed[:, 0]
    crossed = summed[:, 1]
    first_vir = lax.axis_index("blk") * rows_dev
    occ_levels = jnp.take(eps_occ, occ_index)
    own_level = jnp.sum(jnp.where(jnp.arange(occ_count) == occ_row, occ_levels, 0.0))
    vir_levels = lax.dynamic_slice_in_dim(eps_vir, first_vir, rows_dev, 0)
    denominator = (
        own_level + occ_levels[None, :, None] - vir_levels[:, None, None] - eps_vir[None, None, :]
    )
    amplitudes = (direct / denominator)[None]
    pair_part = jnp.sum(direct * (2.0 * direct - crossed) / denominator, axis=(0, 2))
    pair_energy = lax.psum(pair_part, "blk")[None]
    return (amplitudes, pair_energy)


def solution(mesh):
    in_specs = (
        P(("aux", "blk"), None, None, None),
        P(("aux", "blk")),
        P(("aux", "blk")),
        P(("aux", "blk")),
        P(),
        P(),
        P(),
        P(),
    )
    out_specs = (P("aux", "blk", None, None), P("aux", None))
    return jax.shard_map(body, mesh=mesh, in_specs=in_specs, out_specs=out_specs, check_vma=False)
```

profile of v0, /device:TPU:0, one launch (start us, length us, event | category | flops | bytes accessed | tf_op | source)
XLA Modules:
  0.0 131.5 jit_solution(10336060481008152967)
XLA Ops:
  7.2 0.0 copy-start
  7.2 0.0 all-gather.2.cloned.1.call-start
  7.2 0.8 compare_select_fusion.1
  8.0 0.8 compare_and_fusion
  8.8 0.3 copy-done
  9.1 1.5 %gather_fusion = bf16[12,128,256]{2,1,0:T(8,128)(2,1)} fusion(bf16[48,128,256]{2,1,0:T(8,128)(2,1)S(1)} %bitcast.68, s32[1024]{0:T(1024)S(1)} %pad_clamp_fusion.1), kind=kCustom, calls=%fused_computation | custom fusion | bytes 1572912 | tf_op jit(solution)/shard_map/jit(_take)/gather | solution.py:17
  10.6 4.8 %convolution_bitcast_fusion = bf16[12,4,128,256]{2,3,1,0:T(8,128)(2,1)} fusion(bf16[12,4,128,128]{3,2,1,0:T(8,128)(2,1)} %param.8, bf16[12,128,256]{2,1,0:T(8,128)(2,1)} %gather_fusion, pred[12]{0:T(512)(128)(4,1)S(1)} %compare_and_fusion), kind=kOutput, calls=%fused_computation.2 | convolution fusion | flops 403046400 | bytes 5505036 | tf_op jit(solution)/shard_map/soqn,snv->soqv/dot_general | solution.py:18
  15.4 0.0 copy-start.4
  15.4 7.7 %copy.28 = bf16[12,4,128,256]{3,0,2,1:T(8,128)(2,1)} copy(bf16[12,4,128,256]{2,3,1,0:T(8,128)(2,1)} %convolution_bitcast_fusion) | data formatting | bytes 6291456 | tf_op jit(solution)/shard_map/soqn,snv->soqv/dot_general | solution.py:18
  23.7 0.0 copy-done.4
  23.7 2.9 %fusion = bf16[2,128,4,256]{3,0,1,2:T(2,128)(2,1)S(1)} fusion(bf16[12,4,128,256]{3,0,2,1:T(8,128)(2,1)} %copy.28, bf16[12]{0:T(256)(128)(2,1)S(1)} %compare_convert_fusion, s32[12]{0:T(128)S(1)} %copy-done.4), kind=kOutput, calls=%fused_computation.7 | convolution fusion | flops 6291504 | bytes 3670088 | tf_op jit(solution)/shard_map/sk,soqv->kqov/dot_general | solution.py:24
  26.6 0.9 copy.29
  27.5 0.0 all-gather.2.cloned.1.call-update
  27.5 0.0 reduce-scatter.2.cloned.1.call-start
  27.6 38.0 %all-gather.2.cloned.1.call-done = bf16[8,128,4,256]{3,1,2,0:T(8,128)(2,1)} async-done(((bf16[2,128,4,256]{3,1,2,0:T(8,128)(2,1)}), bf16[8,128,4,256]{3,1,2,0:T(8,128)(2,1)}) %all-gather.2.cloned.1.call-update) | async-done | bytes 2097168 | tf_op jit(solution)/shard_map/all_gather | solution.py:25
  65.6 0.0 copy-start.5
  65.6 2.6 %convolution_bitcast_fusion.2 = f32[256,1,4,256]{3,0,2,1:T(8,128)S(1)} fusion(bf16[8,128,4,256]{3,1,2,0:T(8,128)(2,1)} %all-gather.2.cloned.1.call-done, s32[]{:T(128)S(6)} %select_n.33), kind=kOutput, calls=%fused_computation.5 | convolution fusion | flops 536870912 | bytes 3670020 | tf_op jit(solution)/shard_map/dot_general | solution.py:28
  68.2 0.0 copy-done.5
  68.2 0.7 convolution_bitcast_fusion.1
  68.9 1.5 %pad_maximum_fusion = f32[256,2,4,256]{3,0,2,1:T(8,128)} fusion(f32[256,1,4,256]{3,0,2,1:T(8,128)S(1)} %convolution_bitcast_fusion.2, f32[256,1,4,256]{3,0,2,1:T(8,128)S(1)} %convolution_bitcast_fusion.1), kind=kLoop, calls=%fused_computation.3 | loop fusion | flops 524288 | bytes 4194304 | tf_op jit(solution)/shard_map/stack | solution.py:32
  70.4 0.0 copy-start.2
  70.4 0.0 copy-start.3
  70.4 0.0 copy-start.1
  70.4 0.0 reduce-scatter.2.cloned.1.call-update
  70.4 0.6 copy-done.2
  71.1 0.1 dynamic_slice.8
  71.2 0.0 copy-done.3
  71.2 0.0 copy-done.1
  71.2 0.6 gather_fusion.1
  71.8 0.6 fusion.16
  72.4 0.7 broadcast_add_fusion
  73.1 0.1 broadcast_subtract_fusion
  73.2 33.5 %reduce-scatter.2.cloned.1.call-done = f32[32,2,4,256]{3,0,2,1:T(8,128)} async-done(((f32[256,2,4,256]{3,0,2,1:T(8,128)}), f32[32,2,4,256]{3,0,2,1:T(8,128)}) %reduce-scatter.2.cloned.1.call-update) | async-done | bytes 262160 | tf_op jit(solution)/shard_map/reduce_scatter | solution.py:31
  106.7 1.0 bitcast_divide_fusion
  107.7 0.7 copy.34
  108.4 1.2 fusion.12
  109.6 15.1 %psum.7 = f32[1,4]{1,0:T(1,128)} all-reduce(f32[1,4]{1,0:T(1,128)S(1)} %bitcast.69), channel_id=1, replica_groups=mesh['aux'=4,'blk'=8] {'blk'}, use_global_device_ids=true, to_apply=%region_3.4 | all-reduce | flops 4 | bytes 32 | tf_op jit(solution)/shard_map/psum | solution.py:59
  (4 shorter events, 0.0 us)
Async XLA Ops:
  7.2 1.9 %copy-start = (bf16[6144,256]{1,0:T(8,128)(2,1)S(1)}, bf16[6144,256]{1,0:T(8,128)(2,1)}, u32[]{:S(2)}) copy-start(bf16[6144,256]{1,0:T(8,128)(2,1)} %param.12) | copy-start | bytes 9437188
  7.2 58.4 %all-gather.2.cloned.1.call-start = ((), (), s32[]{:S(2)}) async-start(), calls=%async_computation.1 | async-start | bytes 2621440 | tf_op jit(solution)/shard_map/all_gather | solution.py:25
  15.4 8.4 %copy-start.4 = (s32[12]{0:T(128)S(1)}, s32[12]{0:T(128)}, u32[]{:S(2)}) copy-start(s32[12]{0:T(128)} %param.10) | copy-start | bytes 148
  27.5 79.1 %reduce-scatter.2.cloned.1.call-start = ((), (), s32[]{:S(2)}) async-start(), calls=%async_computation.2 | async-start | bytes 2359296 | tf_op jit(solution)/shard_map/reduce_scatter | solution.py:31
  65.6 2.6 %copy-start.5 = (bf16[8,128,4,256]{3,1,2,0:T(8,128)(2,1)S(1)}, bf16[8,128,4,256]{3,1,2,0:T(8,128)(2,1)}, u32[]{:S(2)}) copy-start(bf16[8,128,4,256]{3,1,2,0:T(8,128)(2,1)} %all-gather.2.cloned.1.call-done) | copy-start | bytes 6291460
  70.4 0.7 copy-start.2
  70.4 0.8 copy-start.3
  70.4 0.8 copy-start.1
Sparse Core Ops, SparseCore 0:
  27.6 37.8 all-gather.1
  70.6 36.0 reduce-scatter.1
where the time goes:
time: 132 us; the launch traced here: 131 us
  waiting for transfers between devices  71.6 us (54%)
  blocking collectives  15.1 us (11%)
  between operations  14.8 us (11%)
  local copies, waits for them, and re-layouts  12.5 us (9%)
  matrix products  11 us (8%)
  other arithmetic  6.57 us (5%)
    all_gather x1, waiting for transfers between devices, body(): halfed = lax.all_gather(local_rows, 'aux', axis=0, tiled=True)  38 us
    reduce_scatter x1, waiting for transfers between devices, body(): lax.psum_scatter(jnp.stack([lax.dot_general(own_rows, halfed, (((0, 1), (...  33.5 us
    psum x1, blocking collectives, body(): pair_energy = lax.psum(pair_part, 'blk')[None]  15.1 us
    dot_general x1, local copies, waits for them, and re-layouts, body(): jnp.einsum('soqn,snv->soqv', three_center, coefficients, preferred_elemen...  7.69 us
    dot_general x1, matrix products, body(): jnp.einsum('soqn,snv->soqv', three_center, coefficients, preferred_elemen...  4.8 us
    dot_general x1, matrix products, body(): jnp.einsum('sk,soqv->kqov', select, products).astype(jnp.bfloat16)  2.88 us
  transfers between devices with their start and end apart: 2, of which 2 were waited for; matrix products, arithmetic and copies ran while one was open for 2% of the time, Pallas kernels for 0%

commit v1 on v0

--- a/solution.py
+++ b/solution.py
@@ -22,7 +22,9 @@
     select = (slot_aux[:, None] == jnp.arange(AUX_BLOCKS_DEV)[None, :]).astype(jnp.float32)
     select = select * keep[:, None]
     local_rows = jnp.einsum("sk,soqv->kqov", select, products).astype(jnp.bfloat16)
-    halfed = lax.all_gather(local_rows, "aux", axis=0, tiled=True)
+    halfed = jnp.concatenate(
+        lax.all_to_all(jnp.stack([local_rows] * lax.axis_size("aux")), "aux", 0, 0), axis=0
+    )
     own_rows = lax.dynamic_index_in_dim(halfed, occ_row, 2, keepdims=False)
     rows_dev = vir_count // blk_count
     mixed = lax.dot_general(

time: 132 us -> 126 us (0.955)
  waiting for transfers between devices: 71.6 us -> 59.7 us
  starting transfers between devices: 0.08 us -> 5.19 us
  local copies, waits for them, and re-layouts: 12.5 us -> 14.9 us
  matrix products: 11 us -> 9.16 us
    all_gather x1 -> x0, waiting for transfers between devices: 38 us -> none  [body(): halfed = lax.all_gather(local_rows, 'aux', axis=0, tiled=True)]
    all_to_all x0 -> x1, waiting for transfers between devices: none -> 25.7 us  [body(): lax.all_to_all(jnp.stack([local_rows] * lax.axis_size('aux')), 'aux', 0, 0)]
    all_to_all x0 -> x1, starting transfers between devices: none -> 5.19 us  [body(): lax.all_to_all(jnp.stack([local_rows] * lax.axis_size('aux')), 'aux', 0, 0)]
    dot_general x1, matrix products: 2.57 us -> 0.74 us  [body(): lax.dot_general(halfed, own_rows, (((0, 1), (0, 1)), ((), ())), preferred...]
    all_to_all x0 -> x1, local copies, waits for them, and re-layouts: none -> 1.73 us  [body(): lax.all_to_all(jnp.stack([local_rows] * lax.axis_size('aux')), 'aux', 0, 0)]
    another operation x0 -> x1, local copies, waits for them, and re-layouts: none -> 1.53 us  [body(): jnp.stack([local_rows] * lax.axis_size('aux'))]
where the time goes in v1:
time: 126 us
  waiting for transfers between devices  59.7 us (47%)
  blocking collectives  15.2 us (12%)
  local copies, waits for them, and re-layouts  14.9 us (12%)
  between operations  14.8 us (12%)
  matrix products  9.16 us (7%)
  other arithmetic  6.62 us (5%)
  starting transfers between devices  5.19 us (4%)
    reduce_scatter x1, waiting for transfers between devices, body(): lax.psum_scatter(jnp.stack([lax.dot_general(own_rows, halfed, (((0, 1), (...  34 us
    all_to_all x1, waiting for transfers between devices, body(): lax.all_to_all(jnp.stack([local_rows] * lax.axis_size('aux')), 'aux', 0, 0)  25.7 us
    psum x1, blocking collectives, body(): pair_energy = lax.psum(pair_part, 'blk')[None]  15.2 us
    dot_general x1, local copies, waits for them, and re-layouts, body(): jnp.einsum('soqn,snv->soqv', three_center, coefficients, preferred_elemen...  7.7 us
    all_to_all x1, starting transfers between devices, body(): lax.all_to_all(jnp.stack([local_rows] * lax.axis_size('aux')), 'aux', 0, 0)  5.19 us
    dot_general x1, matrix products, body(): jnp.einsum('soqn,snv->soqv', three_center, coefficients, preferred_elemen...  4.8 us
    dot_general x1, matrix products, body(): jnp.einsum('sk,soqv->kqov', select, products).astype(jnp.bfloat16)  2.88 us
  transfers between devices with their start and end apart: 2, of which 2 were waited for; matrix products, arithmetic and copies ran while one was open for 2% of the time, Pallas kernels for 0%

profile of v1, /device:TPU:0, one launch (start us, length us, event | category | flops | bytes accessed | tf_op | source)
XLA Modules:
  0.0 125.5 jit_solution(9324164239250035023)
XLA Ops:
  7.2 0.0 copy-start
  7.2 0.8 compare_select_fusion.1
  8.0 0.8 compare_and_fusion
  8.8 0.3 copy-done
  9.1 1.5 %gather_fusion = bf16[12,128,256]{2,1,0:T(8,128)(2,1)} fusion(bf16[48,128,256]{2,1,0:T(8,128)(2,1)S(1)} %bitcast.61, s32[1024]{0:T(1024)S(1)} %pad_clamp_fusion.1), kind=kCustom, calls=%fused_computation | custom fusion | bytes 1572912 | tf_op jit(solution)/shard_map/jit(_take)/gather | solution.py:17
  10.6 4.8 %convolution_bitcast_fusion = bf16[12,4,128,256]{2,3,1,0:T(8,128)(2,1)} fusion(bf16[12,4,128,128]{3,2,1,0:T(8,128)(2,1)} %param.8, bf16[12,128,256]{2,1,0:T(8,128)(2,1)} %gather_fusion, pred[12]{0:T(512)(128)(4,1)S(1)} %compare_and_fusion), kind=kOutput, calls=%fused_computation.2 | convolution fusion | flops 403046400 | bytes 5505036 | tf_op jit(solution)/shard_map/soqn,snv->soqv/dot_general | solution.py:18
  15.4 0.0 copy-start.4
  15.4 7.7 %copy.25 = bf16[12,4,128,256]{3,0,2,1:T(8,128)(2,1)} copy(bf16[12,4,128,256]{2,3,1,0:T(8,128)(2,1)} %convolution_bitcast_fusion) | data formatting | bytes 6291456 | tf_op jit(solution)/shard_map/soqn,snv->soqv/dot_general | solution.py:18
  23.7 0.0 copy-done.4
  23.7 2.9 %fusion = bf16[2,128,4,256]{3,0,1,2:T(2,128)(2,1)S(1)} fusion(bf16[12,4,128,256]{3,0,2,1:T(8,128)(2,1)} %copy.25, bf16[12]{0:T(256)(128)(2,1)S(1)} %compare_convert_fusion, s32[12]{0:T(128)S(1)} %copy-done.4), kind=kOutput, calls=%fused_computation.7 | convolution fusion | flops 6291504 | bytes 3670088 | tf_op jit(solution)/shard_map/sk,soqv->kqov/dot_general | solution.py:24
  26.6 0.1 copy.26
  26.7 1.5 %stack.16 = bf16[4,2,128,4,256]{4,2,1,3,0:T(8,128)(2,1)} broadcast(bf16[2,128,4,256]{3,1,0,2:T(8,128)(2,1)S(1)} %copy.26), dimensions={1,2,3,4} | broadcast | bytes 2621440 | tf_op jit(solution)/shard_map/stack | solution.py:26
  28.3 5.2 %all-to-all-start = ((bf16[4,2,128,4,256]{4,2,1,3,0:T(8,128)(2,1)}), bf16[4,2,128,4,256]{4,2,1,3,0:T(8,128)(2,1)}, u32[]{:S(2)}, u32[]{:S(2)}) async-start(bf16[4,2,128,4,256]{4,2,1,3,0:T(8,128)(2,1)} %stack.16), calls=%async_computation | async-start | bytes 4194304 | tf_op jit(solution)/shard_map/all_to_all | solution.py:26
  33.4 0.0 reduce-scatter.2.cloned.1.call-start
  33.4 25.7 %all-to-all-done = bf16[4,2,128,4,256]{4,2,1,3,0:T(8,128)(2,1)} async-done(((bf16[4,2,128,4,256]{4,2,1,3,0:T(8,128)(2,1)}), bf16[4,2,128,4,256]{4,2,1,3,0:T(8,128)(2,1)}, u32[]{:S(2)}, u32[]{:S(2)}) %all-to-all-start) | async-done | bytes 2097184 | tf_op jit(solution)/shard_map/all_to_all | solution.py:26
  59.2 1.7 %copy.27 = bf16[4,2,128,4,256]{4,2,1,0,3:T(8,128)(2,1)S(1)} copy(bf16[4,2,128,4,256]{4,2,1,3,0:T(8,128)(2,1)} %all-to-all-done) | data formatting | bytes 4194304 | tf_op jit(solution)/shard_map/all_to_all | solution.py:26
  60.9 0.7 convolution_bitcast_fusion.1
  61.7 0.7 convolution_bitcast_fusion.2
  62.4 1.5 %pad_maximum_fusion = f32[256,2,4,256]{3,0,2,1:T(8,128)} fusion(f32[256,1,4,256]{3,0,2,1:T(8,128)S(1)} %convolution_bitcast_fusion.1, f32[256,1,4,256]{3,0,2,1:T(8,128)S(1)} %convolution_bitcast_fusion.2), kind=kLoop, calls=%fused_computation.3 | loop fusion | flops 524288 | bytes 4194304 | tf_op jit(solution)/shard_map/stack | solution.py:34
  63.9 0.0 copy-start.2
  63.9 0.0 copy-start.3
  63.9 0.0 copy-start.1
  63.9 0.0 reduce-scatter.2.cloned.1.call-update
  63.9 0.6 copy-done.2
  64.6 0.1 dynamic_slice.8
  64.6 0.0 copy-done.3
  64.7 0.0 copy-done.1
  64.7 0.6 gather_fusion.1
  65.3 0.6 fusion.16
  65.9 0.7 broadcast_add_fusion
  66.6 0.1 broadcast_subtract_fusion
  66.6 34.0 %reduce-scatter.2.cloned.1.call-done = f32[32,2,4,256]{3,0,2,1:T(8,128)} async-done(((f32[256,2,4,256]{3,0,2,1:T(8,128)}), f32[32,2,4,256]{3,0,2,1:T(8,128)}) %reduce-scatter.2.cloned.1.call-update) | async-done | bytes 262160 | tf_op jit(solution)/shard_map/reduce_scatter | solution.py:33
  100.6 1.0 bitcast_divide_fusion
  101.6 0.7 copy.30
  102.4 1.2 fusion.12
  103.5 15.2 %psum.7 = f32[1,4]{1,0:T(1,128)} all-reduce(f32[1,4]{1,0:T(1,128)S(1)} %bitcast.64), channel_id=1, replica_groups=mesh['aux'=4,'blk'=8] {'blk'}, use_global_device_ids=true, to_apply=%region_3.4 | all-reduce | flops 4 | bytes 32 | tf_op jit(solution)/shard_map/psum | solution.py:61
  (4 shorter events, 0.0 us)
Async XLA Ops:
  7.2 1.9 %copy-start = (bf16[6144,256]{1,0:T(8,128)(2,1)S(1)}, bf16[6144,256]{1,0:T(8,128)(2,1)}, u32[]{:S(2)}) copy-start(bf16[6144,256]{1,0:T(8,128)(2,1)} %param.12) | copy-start | bytes 9437188
  15.4 8.4 %copy-start.4 = (s32[12]{0:T(128)S(1)}, s32[12]{0:T(128)}, u32[]{:S(2)}) copy-start(s32[12]{0:T(128)} %param.10) | copy-start | bytes 148
  28.3 30.9 %all-to-all-start = ((bf16[4,2,128,4,256]{4,2,1,3,0:T(8,128)(2,1)}), bf16[4,2,128,4,256]{4,2,1,3,0:T(8,128)(2,1)}, u32[]{:S(2)}, u32[]{:S(2)}) async-start(bf16[4,2,128,4,256]{4,2,1,3,0:T(8,128)(2,1)} %stack.16), calls=%async_computation | async-start | bytes 4194304 | tf_op jit(solution)/shard_map/all_to_all | solution.py:26
  33.4 67.2 %reduce-scatter.2.cloned.1.call-start = ((), (), s32[]{:S(2)}) async-start(), calls=%async_computation.2 | async-start | bytes 2359296 | tf_op jit(solution)/shard_map/reduce_scatter | solution.py:33
  63.9 0.7 copy-start.2
  63.9 0.8 copy-start.3
  63.9 0.8 copy-start.1
Sparse Core Ops, SparseCore 0:
  64.0 36.5 reduce-scatter.1
